TPU v7x, 256 devices: a whole 4x4x8 slice. The times are simulated.
256 devices in a mesh: leaf: 8 (over y, core), front: 32 (over x, z).
Axes of the slice: x: 4, y: 4, z: 8, core: 2. Of those that a mesh axis runs over, the one named last changes fastest.
Arguments:
- child_fronts: float32 [8, 4096, 1, 32, 128], P('leaf', None, None, 'front'), as said below
- parent_front: float32 [8, 8, 128, 2, 32, 128], P(None, 'leaf', None, None, 'front'), as said below
- child_map: int32 [8, 24], replicated, may hold values from 0 to 63, as said below
Outputs:
- child_result: float32 [8, 4096, 1, 32, 128], P('leaf', None, None, 'front')
- parent_result: float32 [8, 8, 128, 2, 32, 128], P(None, 'leaf', None, None, 'front')
Inputs may be any that keep to these rules, and one draw needn't show every extreme that they name: Row g gives, for each update block v of child g, the parent block that receives it. The entries of a row are distinct, child_map[g, v] mod 32 equals (8 + v) mod 32, and every child's last update block goes to the parent's last block. `child_fronts`: each front is symmetric positive definite. `parent_front`: the parent front is symmetric positive definite.
All inputs are finite; a program needn't handle non-finite values.
Results may differ from a plain program's by a relative error of at most 0.000059.
Values sent between devices are 32-bit elements; how exact they have to be, the bound alone decides.
No kernel may reach another device: no remote copies, remote signals or barrier semaphores. Data moves between devices by JAX's collectives and lax.ppermute only.
A program may use at most 256 MiB of HBM per device.

v0:
```python
import jax
import jax.numpy as jnp
from jax import lax
from jax.sharding import PartitionSpec as P

CHILD_PIVOTS = 8
PARENT_PIVOTS = 2


def from_root(value, axis, source):
    kept = jnp.where(lax.axis_index(axis) == source, value, 0).astype(value.dtype)
    return lax.psum(kept, axis)


def solve_rows(factor, rows):
    return jax.scipy.linalg.solve_triangular(factor, rows.T, lower=True).T


def body(child_fronts, parent_front, child_map):
    front_count = lax.axis_size("front")
    leaf_count = lax.axis_size("leaf")
    front_pos = lax.axis_index("front")
    leaf_pos = lax.axis_index("leaf")
    block = child_fronts.shape[4]
    child_order = child_fronts.shape[1]
    child_slots = child_fronts.shape[2]
    blocks_total = child_order // block
    pivots = CHILD_PIVOTS
    highest = lax.Precision.HIGHEST
    matrix = child_fronts.reshape(child_order, child_slots * block)
    column_ids = jnp.arange(child_slots * block) // block * front_count + front_pos
    slot_ids = jnp.arange(child_slots) * front_count + front_pos
    panel_slots = (pivots + front_count - 1) // front_count
    piece_rows = child_order // front_count
    width = pivots * block
    leading = matrix.reshape(front_count, piece_rows, panel_slots, 1, block)
    spread = lax.all_to_all(leading, "front", split_axis=0, concat_axis=3, tiled=True)
    rows_part = spread.reshape(piece_rows, panel_slots * front_count * block)[:, :width]
    panel = lax.all_gather(rows_part, "front", axis=0, tiled=True)
    factored = []
    for pivot in range(pivots):
        start = pivot * block
        finish = start + block
        current = panel[:, start:finish]
        if factored:
            done = jnp.concatenate(factored, 1)
            current = current - jnp.dot(done, done[start:finish].T, precision=highest)
        factor = jnp.linalg.cholesky(current[start:finish])
        below = solve_rows(factor, current[finish:])
        factored.append(jnp.concatenate([jnp.zeros((start, block), jnp.float32), factor, below], 0))
    panel = jnp.concatenate(factored, 1)
    lower_rows = panel[width:]
    padded = jnp.concatenate([jnp.zeros((width, width), jnp.float32), lower_rows], 0)
    picked = jnp.take(padded.reshape(blocks_total, block, width), slot_ids, axis=0)
    picked = picked.reshape(child_slots * block, width)
    update = jnp.dot(lower_rows, picked.T, precision=highest)
    matrix = jnp.concatenate([matrix[:width], matrix[width:] - update], 0)
    pivot_columns = jnp.take(
        panel.reshape(child_order, pivots, block), jnp.clip(slot_ids, 0, pivots - 1), axis=1
    )
    pivot_columns = pivot_columns.reshape(child_order, child_slots * block)
    matrix = jnp.where((column_ids < pivots)[None, :], pivot_columns, matrix)
    row_blocks = jnp.arange(child_order) // block
    matrix = jnp.where(
        (row_blocks[:, None] < pivots) & (column_ids[None, :] >= pivots), 0.0, matrix
    )
    child_result = matrix.reshape(child_fronts.shape)
    first_slot = pivots // front_count
    update_count = blocks_total - pivots
    quota = update_count // leaf_count
    kept_slots = child_slots - first_slot
    outgoing = matrix[pivots * block :, first_slot * block :].reshape(
        quota, leaf_count, block, kept_slots, block
    )
    received = lax.all_to_all(outgoing, "leaf", split_axis=1, concat_axis=1, tiled=True)
    parent_rslots = parent_front.shape[0]
    parent_cslots = parent_front.shape[3]
    groups = child_map.shape[0]
    row_map = lax.dynamic_index_in_dim(
        child_map.reshape(groups, quota, leaf_count), leaf_pos, axis=2, keepdims=False
    )
    row_onehot = (
        (row_map // leaf_count)[:, :, None] == jnp.arange(parent_rslots)[None, None, :]
    ).astype(jnp.float32)
    col_blocks = jnp.arange(first_slot, child_slots) * front_count + front_pos - pivots
    valid = col_blocks >= 0
    col_map = jnp.take(child_map, jnp.clip(col_blocks, 0, update_count - 1), axis=1)
    col_match = (col_map // front_count)[:, :, None] == jnp.arange(parent_cslots)[None, None, :]
    col_onehot = (valid[None, :, None] & col_match).astype(jnp.float32)
    placed = jnp.einsum("gqa,qgxcy->gaxcy", row_onehot, received, precision=highest)
    summed = jnp.einsum("gcb,gaxcy->axby", col_onehot, placed, precision=highest)
    parent = parent_front.reshape(parent_rslots * block, parent_cslots * block)
    parent = parent + summed.reshape(parent_rslots * block, parent_cslots * block)
    prow_ids = jnp.arange(parent_rslots * block) // block * leaf_count + leaf_pos
    pcol_ids = jnp.arange(parent_cslots * block) // block * front_count + front_pos
    col_slot_ids = jnp.arange(parent_cslots) * front_count + front_pos
    parent_blocks = parent_rslots * leaf_count
    for pivot in range(PARENT_PIVOTS):
        col_root = pivot % front_count
        col_slot = pivot // front_count
        column = from_root(parent[:, col_slot * block : (col_slot + 1) * block], "front", col_root)
        whole = lax.all_gather(
            column.reshape(parent_rslots, 1, block, block), "leaf", axis=1, tiled=True
        )
        whole = whole.reshape(parent_blocks * block, block)
        factor = jnp.linalg.cholesky(whole[pivot * block : (pivot + 1) * block])
        above = jnp.arange(parent_blocks * block) // block <= pivot
        panel_all = jnp.where(above[:, None], 0.0, solve_rows(factor, whole))
        panel_local = lax.dynamic_index_in_dim(
            panel_all.reshape(parent_rslots, leaf_count, block, block),
            leaf_pos,
            axis=1,
            keepdims=False,
        )
        panel_local = panel_local.reshape(parent_rslots * block, block)
        panel_cols = jnp.take(panel_all.reshape(parent_blocks, block, block), col_slot_ids, axis=0)
        panel_cols = panel_cols.reshape(parent_cslots * block, block)
        parent = parent - jnp.dot(panel_local, panel_cols.T, precision=highest)
        new_column = jnp.where(
            (prow_ids == pivot)[:, None], jnp.tile(factor, (parent_rslots, 1)), panel_local
        )
        parent = jnp.where(
            (pcol_ids == pivot)[None, :], jnp.tile(new_column, (1, parent_cslots)), parent
        )
    parent = jnp.where(
        (prow_ids[:, None] < PARENT_PIVOTS) & (pcol_ids[None, :] >= PARENT_PIVOTS), 0.0, parent
    )
    parent_result = parent.reshape(parent_front.shape)
    return (child_result, parent_result)


def solution(mesh):
    return jax.shard_map(
        body,
        mesh=mesh,
        in_specs=(
            P("leaf", None, None, "front", None),
            P(None, "leaf", None, None, "front", None),
            P(),
        ),
        out_specs=(
            P("leaf", None, None, "front", None),
            P(None, "leaf", None, None, "front", None),
        ),
        check_vma=False,
    )
```

profile of v0, /device:TPU:1, one launch (start us, length us, event | category | flops | bytes accessed | tf_op | source)
XLA Modules:
  0.0 1122.5 jit_solution(9140086913253102955)
XLA Ops:
  9.1 58.8 %all_to_all.20 = f32[32,128,1,1,128]{1,4,3,2,0:T(8,128)S(1)} all-to-all(f32[32,128,1,1,128]{1,4,3,2,0:T(8,128)S(1)} %copy.144), channel_id=1, replica_groups=mesh['leaf'=8,'front'=32] {'front'}, dimensions={0} | all-to-all | bytes 4194304 | tf_op jit(solution)/shard_map/all_to_all | solution.py:37
  70.8 147.3 %all-gather.4.cloned.1.call-done = f32[4096,1024]{0,1:T(8,128)} async-done(((f32[128,1024]{0,1:T(8,128)}), f32[4096,1024]{0,1:T(8,128)}) %all-gather.4.cloned.1.call-update) | async-done | bytes 16777232 | tf_op jit(solution)/shard_map/all_gather | solution.py:39
  219.9 11.7 %cholesky.164 = f32[128,128]{1,0:T(8,128)S(1)} custom-call(f32[128,128]{1,0:T(8,128)S(1)} %fusion.173), custom_call_target="Cholesky" | custom-call | tf_op jit(solution)/shard_map/jit(cholesky)/cholesky | solution.py:48
  233.0 9.8 custom-call.37
  256.6 11.9 %cholesky.175 = f32[128,128]{1,0:T(8,128)S(1)} custom-call(f32[128,128]{1,0:T(8,128)S(1)} %fusion.171), custom_call_target="Cholesky" | custom-call | tf_op jit(solution)/shard_map/jit(cholesky)/cholesky | solution.py:48
  269.8 9.8 custom-call.38
  284.5 4.8 convolution_subtract_fusion.2
  291.5 12.1 %cholesky.186 = f32[128,128]{1,0:T(8,128)S(1)} custom-call(f32[128,128]{1,0:T(8,128)S(1)} %fusion.169), custom_call_target="Cholesky" | custom-call | tf_op jit(solution)/shard_map/jit(cholesky)/cholesky | solution.py:48
  305.0 9.8 custom-call.39
  319.5 7.6 fusion.38
  329.4 11.7 %cholesky.197 = f32[128,128]{1,0:T(8,128)S(1)} custom-call(f32[128,128]{1,0:T(8,128)S(1)} %fusion.167), custom_call_target="Cholesky" | custom-call | tf_op jit(solution)/shard_map/jit(cholesky)/cholesky | solution.py:48
  342.5 9.8 custom-call.40
  357.0 10.2 fusion.41
  369.6 11.7 %cholesky.208 = f32[128,128]{1,0:T(8,128)S(1)} custom-call(f32[128,128]{1,0:T(8,128)S(1)} %fusion.165), custom_call_target="Cholesky" | custom-call | tf_op jit(solution)/shard_map/jit(cholesky)/cholesky | solution.py:48
  382.6 9.8 custom-call.41
  414.2 10.0 convolution_subtract_fusion.1
  424.3 11.7 %cholesky.219 = f32[128,128]{1,0:T(8,128)S(1)} custom-call(f32[128,128]{1,0:T(8,128)S(1)} %fusion.163), custom_call_target="Cholesky" | custom-call | tf_op jit(solution)/shard_map/jit(cholesky)/cholesky | solution.py:48
  437.4 9.8 custom-call.42
  450.1 4.8 fusion.79
  454.9 10.7 convolution_subtract_fusion
  465.7 11.7 %cholesky.230 = f32[128,128]{1,0:T(8,128)S(1)} custom-call(f32[128,128]{1,0:T(8,128)S(1)} %fusion.161), custom_call_target="Cholesky" | custom-call | tf_op jit(solution)/shard_map/jit(cholesky)/cholesky | solution.py:48
  478.8 9.8 custom-call.43
  495.4 12.9 %convolution_subtract_fusion.4 = f32[4096,128]{0,1:T(8,128)S(1)} fusion(f32[4096,896]{0,1:T(8,128)} %get-tuple-element.91, f32[4096,1024]{0,1:T(8,128)} %all-gather.4.cloned.1.call-done), kind=kOutput, calls=%fused_computation.48 | convolution fusion | flops 5637668864 | bytes 19333120 | tf_op jit(solution)/shard_map/dot_general | solution.py:47
  508.4 11.7 %cholesky.241 = f32[128,128]{1,0:T(8,128)S(1)} custom-call(f32[128,128]{1,0:T(8,128)S(1)} %fusion.159), custom_call_target="Cholesky" | custom-call | tf_op jit(solution)/shard_map/jit(cholesky)/cholesky | solution.py:48
  521.5 9.8 custom-call.44
  537.0 10.8 slice.282
  547.8 7.4 pad_bitcast_fusion
  555.2 8.9 copy.226
  566.9 21.1 %convolution_subtract_fusion.5 = f32[3072,128]{1,0:T(8,128)} fusion(f32[128,1024]{0,1:T(8,128)S(1)} %bitcast.252, f32[1,4096,1,1,128]{4,1,3,2,0:T(8,128)S(1)} %bitcast.235, f32[4096,1024]{0,1:T(8,128)S(1)} %bitcast.221), kind=kOutput, calls=%fused_computation.66 | convolution fusion | flops 4832231424 | bytes 16252928 | tf_op jit(solution)/shard_map/dot_general | solution.py:56
  595.6 7.6 all-to-all-start.1
  604.2 19.8 %all-to-all-done.1 = f32[3,8,128,1,128]{4,2,0,3,1:T(8,128)} async-done(((f32[3,8,128,1,128]{4,2,0,3,1:T(8,128)}), f32[3,8,128,1,128]{4,2,0,3,1:T(8,128)}, u32[]{:S(2)}, u32[]{:S(2)}) %all-to-all-start.1) | async-done | bytes 1572896 | tf_op jit(solution)/shard_map/all_to_all | solution.py:75
  635.1 138.2 %all-reduce.4.cloned.1.call-done = f32[8,1,128,128]{3,2,0,1:T(8,128)} async-done(((f32[8,1,128,128]{3,2,0,1:T(8,128)}), f32[8,1,128,128]{3,2,0,1:T(8,128)}) %all-reduce.4.cloned.1.call-update) | async-done | bytes 524304 | tf_op jit(solution)/shard_map/psum | solution.py:12
  773.6 38.3 %all-gather.6.cloned.1.call-done = f32[8,8,128,128]{3,2,0,1:T(8,128)} async-done(((f32[8,1,128,128]{3,2,0,1:T(8,128)}), f32[8,8,128,128]{3,2,0,1:T(8,128)}) %all-gather.6.cloned.1.call-update) | async-done | bytes 4194320 | tf_op jit(solution)/shard_map/all_gather | solution.py:102
  811.9 5.4 copy.184
  817.4 5.5 copy.254
  825.8 11.7 %cholesky.252 = f32[128,128]{1,0:T(8,128)S(1)} custom-call(f32[128,128]{1,0:T(8,128)S(1)} %fusion.157), custom_call_target="Cholesky" | custom-call | tf_op jit(solution)/shard_map/jit(cholesky)/cholesky | solution.py:106
  838.8 9.8 custom-call.46
  848.6 8.6 convolution_select_fusion.1
  860.1 5.8 copy.210
  872.6 142.5 %all-reduce.6.cloned.1.call-done = f32[8,1,128,128]{3,2,0,1:T(8,128)} async-done(((f32[8,1,128,128]{3,2,0,1:T(8,128)}), f32[8,1,128,128]{3,2,0,1:T(8,128)}) %all-reduce.6.cloned.1.call-update) | async-done | bytes 524304 | tf_op jit(solution)/shard_map/psum | solution.py:12
  1015.2 5.3 fusion.57
  1020.6 33.0 %all-gather.8.cloned.1.call-done = f32[8,8,128,128]{3,2,0,1:T(8,128)} async-done(((f32[8,1,128,128]{3,2,0,1:T(8,128)}), f32[8,8,128,128]{3,2,0,1:T(8,128)}) %all-gather.8.cloned.1.call-update) | async-done | bytes 4194320 | tf_op jit(solution)/shard_map/all_gather | solution.py:102
  1053.5 5.4 copy.188
  1058.9 5.5 copy.253
  1067.3 11.7 %cholesky.263 = f32[128,128]{1,0:T(8,128)S(1)} custom-call(f32[128,128]{1,0:T(8,128)S(1)} %fusion.155), custom_call_target="Cholesky" | custom-call | tf_op jit(solution)/shard_map/jit(cholesky)/cholesky | solution.py:106
  1080.4 9.8 custom-call.47
  1090.2 8.7 convolution_select_fusion
  1101.7 5.6 copy.211
  (204 shorter events, 141.0 us)
Async XLA Ops:
  7.2 211.0 %all-gather.4.cloned.1.call-start = ((), (), s32[]{:S(2)}) async-start(), calls=%async_computation.2 | async-start | bytes 17301504 | tf_op jit(solution)/shard_map/all_gather | solution.py:39
  68.9 177.4 %copy-start.17 = (pred[4096]{0:T(1024)(128)(4,1)}, pred[4096]{0:T(1024)(128)(4,1)S(1)}, u32[]{:S(2)}) copy-start(pred[4096]{0:T(1024)(128)(4,1)S(1)} %fusion.195) | copy-start | bytes 12292
  254.3 1.3 copy-start.5
  289.2 1.3 copy-start.6
  327.1 1.3 copy-start.14
  367.1 1.3 copy-start.15
  368.6 28.3 %copy-start.2 = (f32[3840,128]{0,1:T(8,128)S(1)}, f32[3840,128]{0,1:T(8,128)}, u32[]{:S(2)}) copy-start(f32[3840,128]{0,1:T(8,128)} %fusion.62) | copy-start | bytes 5898244
  396.9 4.4 copy-start.7
  401.3 4.3 copy-start.8
  405.6 4.2 copy-start.9
  547.8 19.0 %slice-start = ((s8[16777216]{0:T(1024)(128)(4,1)}), s8[4194304]{0:T(1024)(128)(4,1)S(1)}, s32[]{:S(2)}) async-start(s8[16777216]{0:T(1024)(128)(4,1)} %bitcast.220), calls=%async_computation.7 | async-start | bytes 8388608
  547.8 19.0 %slice-start.1 = ((s8[16777216]{0:T(1024)(128)(4,1)}), s8[4194304]{0:T(1024)(128)(4,1)S(1)}, s32[]{:S(2)}) async-start(s8[16777216]{0:T(1024)(128)(4,1)} %bitcast.220), calls=%async_computation.8 | async-start | bytes 8388608
  555.2 11.6 %slice-start.2 = ((s8[16777216]{0:T(1024)(128)(4,1)}), s8[4194304]{0:T(1024)(128)(4,1)S(1)}, s32[]{:S(2)}) async-start(s8[16777216]{0:T(1024)(128)(4,1)} %bitcast.220), calls=%async_computation.9 | async-start | bytes 8388608
  555.2 11.6 %slice-start.3 = ((s8[16777216]{0:T(1024)(128)(4,1)}), s8[4194304]{0:T(1024)(128)(4,1)S(1)}, s32[]{:S(2)}) async-start(s8[16777216]{0:T(1024)(128)(4,1)} %bitcast.220), calls=%async_computation.10 | async-start | bytes 8388608
  555.2 11.6 %copy-start.4 = (f32[1,4096,1,1,128]{4,3,2,1,0:T(1,128)S(1)}, f32[1,4096,1,1,128]{4,3,2,1,0:T(1,128)}, u32[]{:S(2)}) copy-start(f32[1,4096,1,1,128]{4,3,2,1,0:T(1,128)} %param.8) | copy-start | bytes 6291460
  591.4 1.4 copy-start.3
  591.4 1.4 slice-start.4
  595.6 8.0 copy-start.19
  595.6 28.4 %all-to-all-start.1 = ((f32[3,8,128,1,128]{4,2,0,3,1:T(8,128)}), f32[3,8,128,1,128]{4,2,0,3,1:T(8,128)}, u32[]{:S(2)}, u32[]{:S(2)}) async-start(f32[3,8,128,1,128]{4,2,0,3,1:T(8,128)} %copy.181), calls=%async_computation.1 | async-start | bytes 3145728 | tf_op jit(solution)/shard_map/all_to_all | solution.py:75
  603.2 170.1 %all-reduce.4.cloned.1.call-start = ((), (), s32[]{:S(2)}) async-start(), calls=%async_computation.3 | async-start | bytes 1048576 | tf_op jit(solution)/shard_map/psum | solution.py:12
  628.8 4.3 copy-start.16
  633.2 1.0 copy-start.10
  635.1 176.9 %all-gather.6.cloned.1.call-start = ((), (), s32[]{:S(2)}) async-start(), calls=%async_computation.4 | async-start | bytes 4718592 | tf_op jit(solution)/shard_map/all_gather | solution.py:102
  773.3 241.9 %all-reduce.6.cloned.1.call-start = ((), (), s32[]{:S(2)}) async-start(), calls=%async_computation.5 | async-start | bytes 1048576 | tf_op jit(solution)/shard_map/psum | solution.py:12
  822.8 2.0 copy-start.12
  857.2 1.9 copy-start.1
  860.1 8.6 copy-start.11
  869.3 145.9 %copy-start.18 = (pred[4096]{0:T(1024)(128)(4,1)S(1)}, pred[4096]{0:T(1024)(128)(4,1)}, u32[]{:S(2)}) copy-start(pred[4096]{0:T(1024)(128)(4,1)} %copy-done.17) | copy-start | bytes 12292
  872.6 180.9 %all-gather.8.cloned.1.call-start = ((), (), s32[]{:S(2)}) async-start(), calls=%async_computation.6 | async-start | bytes 4718592 | tf_op jit(solution)/shard_map/all_gather | solution.py:102
  1064.4 1.9 copy-start.13
  1098.9 1.9 copy-start
Sparse Core Ops, SparseCore 0:
  68.9 149.1 all-gather.3
  635.2 138.0 all-reduce.3
  775.3 36.6 all-gather.5
  872.7 142.3 all-reduce.5
  1016.9 36.6 all-gather.7
where the time goes:
time: 1130 us; the launch traced here: 1120 us
  waiting for transfers between devices  519 us (46%)
  other arithmetic  281 us (25%)
  matrix products  142 us (13%)
  local copies, waits for them, and re-layouts  98.3 us (9%)
  blocking collectives  58.8 us (5%)
  between operations  15.4 us (1%)
    psum x2, waiting for transfers between devices, from_root(): return lax.psum(kept, axis)  281 us
    all_gather x1, waiting for transfers between devices, body(): panel = lax.all_gather(rows_part, 'front', axis=0, tiled=True)  147 us
    another operation x20, other arithmetic, solve_rows(): return jax.scipy.linalg.solve_triangular(factor, rows.T, lower=True).T  105 us
    another operation x24, other arithmetic, body(): factor = jnp.linalg.cholesky(current[start:finish])  99.7 us
    all_gather x2, waiting for transfers between devices, body(): lax.all_gather(column.reshape(parent_rslots, 1, block, block), 'leaf', ax...  71.3 us
    dot_general x7, matrix products, body(): current = current - jnp.dot(done, done[start:finish].T, precision=highest)  59.9 us
    all_to_all x1, blocking collectives, body(): lax.all_to_all(leading, 'front', split_axis=0, concat_axis=3, tiled=True)  58.8 us
    another operation x10, matrix products, solve_rows(): return jax.scipy.linalg.solve_triangular(factor, rows.T, lower=True).T  47.2 us
  transfers between devices with their start and end apart: 6, of which 6 were waited for; matrix products, arithmetic and copies ran while one was open for 1% of the time, Pallas kernels for 0%

commit v1 on v0

--- a/solution.py
+++ b/solution.py
@@ -1,3 +1,4 @@
+import functools
 import jax
 import jax.numpy as jnp
 from jax import lax
@@ -5,6 +6,21 @@
 
 CHILD_PIVOTS = 8
 PARENT_PIVOTS = 2
+
+
+def _arrange_patches(a0, a_name):
+    return jnp.concatenate(
+        lax.all_to_all(
+            jnp.stack([a0 for _ in range(lax.axis_size(a_name))]),
+            axis_name=a_name,
+            split_axis=0,
+            concat_axis=0,
+        ),
+        1,
+    )
+
+
+solve_patch = functools.partial(_arrange_patches, a_name="leaf")
 
 
 def from_root(value, axis, source):
@@ -99,9 +115,7 @@
         col_root = pivot % front_count
         col_slot = pivot // front_count
         column = from_root(parent[:, col_slot * block : (col_slot + 1) * block], "front", col_root)
-        whole = lax.all_gather(
-            column.reshape(parent_rslots, 1, block, block), "leaf", axis=1, tiled=True
-        )
+        whole = solve_patch(column.reshape(parent_rslots, 1, block, block))
         whole = whole.reshape(parent_blocks * block, block)
         factor = jnp.linalg.cholesky(whole[pivot * block : (pivot + 1) * block])
         above = jnp.arange(parent_blocks * block) // block <= pivot

time: 1130 us -> 1170 us (1.035)
  starting transfers between devices: 8.29 us -> 27.7 us
  waiting for transfers between devices: 519 us -> 536 us
    all_to_all x0 -> x2, waiting for transfers between devices: none -> 92.6 us  [_arrange_patches(): lax.all_to_all(jnp.stack([a0 for _ in range(lax.axis_size(a_name))]), axi...]
    all_gather x2 -> x0, waiting for transfers between devices: 71.3 us -> none  [body(): lax.all_gather(column.reshape(parent_rslots, 1, block, block), 'leaf', ax...]
    all_to_all x0 -> x2, starting transfers between devices: none -> 19.7 us  [_arrange_patches(): lax.all_to_all(jnp.stack([a0 for _ in range(lax.axis_size(a_name))]), axi...]
    another operation x0 -> x4, local copies, waits for them, and re-layouts: none -> 15.5 us  [the longest x2 10 us: body(): whole = whole.reshape(parent_blocks * block, block)]
    unnamed x57 -> x51, local copies, waits for them, and re-layouts: 45.1 us -> 30.3 us
    reshape x0 -> x2, local copies, waits for them, and re-layouts: none -> 13.2 us  [_arrange_patches(): jnp.concatenate(lax.all_to_all(jnp.stack([a0 for _ in range(lax.axis_size...]
where the time goes in v1:
time: 1170 us; the launch traced here: 1160 us
  waiting for transfers between devices  536 us (46%)
  other arithmetic  281 us (24%)
  matrix products  136 us (12%)
  local copies, waits for them, and re-layouts  106 us (9%)
  blocking collectives  58.8 us (5%)
  starting transfers between devices  27.7 us (2%)
  between operations  15.3 us (1%)
    psum x2, waiting for transfers between devices, from_root(): return lax.psum(kept, axis)  277 us
    all_gather x1, waiting for transfers between devices, body(): panel = lax.all_gather(rows_part, 'front', axis=0, tiled=True)  147 us
    another operation x20, other arithmetic, solve_rows(): return jax.scipy.linalg.solve_triangular(factor, rows.T, lower=True).T  105 us
    another operation x24, other arithmetic, body(): factor = jnp.linalg.cholesky(current[start:finish])  99.7 us
    all_to_all x2, waiting for transfers between devices, _arrange_patches(): lax.all_to_all(jnp.stack([a0 for _ in range(lax.axis_size(a_name))]), axi...  92.6 us
    dot_general x7, matrix products, body(): current = current - jnp.dot(done, done[start:finish].T, precision=highest)  59.9 us
    all_to_all x1, blocking collectives, body(): lax.all_to_all(leading, 'front', split_axis=0, concat_axis=3, tiled=True)  58.8 us
    another operation x10, matrix products, solve_rows(): return jax.scipy.linalg.solve_triangular(factor, rows.T, lower=True).T  41.1 us
  transfers between devices with their start and end apart: 6, of which 6 were waited for; matrix products, arithmetic and copies ran while one was open for 1% of the time, Pallas kernels for 0%

profile of v1, /device:TPU:1, one launch (start us, length us, event | category | flops | bytes accessed | tf_op | source)
XLA Modules:
  0.0 1160.5 jit_solution(11489920185497049005)
XLA Ops:
  9.1 58.8 %all_to_all.30 = f32[32,128,1,1,128]{1,4,3,2,0:T(8,128)S(1)} all-to-all(f32[32,128,1,1,128]{1,4,3,2,0:T(8,128)S(1)} %copy.146), channel_id=1, replica_groups=mesh['leaf'=8,'front'=32] {'front'}, dimensions={0} | all-to-all | bytes 4194304 | tf_op jit(solution)/shard_map/all_to_all | solution.py:53
  70.8 147.3 %all-gather.2.cloned.1.call-done = f32[4096,1024]{0,1:T(8,128)} async-done(((f32[128,1024]{0,1:T(8,128)}), f32[4096,1024]{0,1:T(8,128)}) %all-gather.2.cloned.1.call-update) | async-done | bytes 16777232 | tf_op jit(solution)/shard_map/all_gather | solution.py:55
  219.9 11.7 %cholesky.164 = f32[128,128]{1,0:T(8,128)S(1)} custom-call(f32[128,128]{1,0:T(8,128)S(1)} %fusion.173), custom_call_target="Cholesky" | custom-call | tf_op jit(solution)/shard_map/jit(cholesky)/cholesky | solution.py:64
  233.0 9.8 custom-call.37
  256.6 11.9 %cholesky.175 = f32[128,128]{1,0:T(8,128)S(1)} custom-call(f32[128,128]{1,0:T(8,128)S(1)} %fusion.171), custom_call_target="Cholesky" | custom-call | tf_op jit(solution)/shard_map/jit(cholesky)/cholesky | solution.py:64
  269.8 9.8 custom-call.38
  291.5 12.1 %cholesky.186 = f32[128,128]{1,0:T(8,128)S(1)} custom-call(f32[128,128]{1,0:T(8,128)S(1)} %fusion.169), custom_call_target="Cholesky" | custom-call | tf_op jit(solution)/shard_map/jit(cholesky)/cholesky | solution.py:64
  305.0 9.8 custom-call.39
  319.5 7.6 fusion.38
  329.4 11.7 %cholesky.197 = f32[128,128]{1,0:T(8,128)S(1)} custom-call(f32[128,128]{1,0:T(8,128)S(1)} %fusion.167), custom_call_target="Cholesky" | custom-call | tf_op jit(solution)/shard_map/jit(cholesky)/cholesky | solution.py:64
  342.5 9.8 custom-call.40
  357.0 10.2 fusion.41
  369.6 11.7 %cholesky.208 = f32[128,128]{1,0:T(8,128)S(1)} custom-call(f32[128,128]{1,0:T(8,128)S(1)} %fusion.165), custom_call_target="Cholesky" | custom-call | tf_op jit(solution)/shard_map/jit(cholesky)/cholesky | solution.py:64
  382.6 9.8 custom-call.41
  414.2 10.0 convolution_subtract_fusion.1
  424.3 11.7 %cholesky.219 = f32[128,128]{1,0:T(8,128)S(1)} custom-call(f32[128,128]{1,0:T(8,128)S(1)} %fusion.163), custom_call_target="Cholesky" | custom-call | tf_op jit(solution)/shard_map/jit(cholesky)/cholesky | solution.py:64
  437.4 9.8 custom-call.42
  454.9 10.7 convolution_subtract_fusion
  465.7 11.7 %cholesky.230 = f32[128,128]{1,0:T(8,128)S(1)} custom-call(f32[128,128]{1,0:T(8,128)S(1)} %fusion.161), custom_call_target="Cholesky" | custom-call | tf_op jit(solution)/shard_map/jit(cholesky)/cholesky | solution.py:64
  478.8 9.8 custom-call.43
  495.4 12.9 %convolution_subtract_fusion.4 = f32[4096,128]{0,1:T(8,128)S(1)} fusion(f32[4096,896]{0,1:T(8,128)} %get-tuple-element.91, f32[4096,1024]{0,1:T(8,128)} %all-gather.2.cloned.1.call-done), kind=kOutput, calls=%fused_computation.48 | convolution fusion | flops 5637668864 | bytes 19333120 | tf_op jit(solution)/shard_map/dot_general | solution.py:63
  508.4 11.7 %cholesky.241 = f32[128,128]{1,0:T(8,128)S(1)} custom-call(f32[128,128]{1,0:T(8,128)S(1)} %fusion.159), custom_call_target="Cholesky" | custom-call | tf_op jit(solution)/shard_map/jit(cholesky)/cholesky | solution.py:64
  521.5 9.8 custom-call.44
  537.0 10.8 slice.282
  547.8 7.4 pad_bitcast_fusion
  555.2 8.9 copy.230
  566.9 21.1 %convolution_subtract_fusion.5 = f32[3072,128]{1,0:T(8,128)} fusion(f32[128,1024]{0,1:T(8,128)S(1)} %bitcast.234, f32[1,4096,1,1,128]{4,1,3,2,0:T(8,128)S(1)} %bitcast.221, f32[4096,1024]{0,1:T(8,128)S(1)} %bitcast.211), kind=kOutput, calls=%fused_computation.64 | convolution fusion | flops 4832231424 | bytes 16252928 | tf_op jit(solution)/shard_map/dot_general | solution.py:72
  595.6 7.6 all-to-all-start.1
  604.2 19.8 %all-to-all-done.1 = f32[3,8,128,1,128]{4,2,0,3,1:T(8,128)} async-done(((f32[3,8,128,1,128]{4,2,0,3,1:T(8,128)}), f32[3,8,128,1,128]{4,2,0,3,1:T(8,128)}, u32[]{:S(2)}, u32[]{:S(2)}) %all-to-all-start.1) | async-done | bytes 1572896 | tf_op jit(solution)/shard_map/all_to_all | solution.py:91
  635.1 138.2 %all-reduce.4.cloned.1.call-done = f32[8,128,128]{2,1,0:T(8,128)} async-done(((f32[8,128,128]{2,1,0:T(8,128)}), f32[8,128,128]{2,1,0:T(8,128)}) %all-reduce.4.cloned.1.call-update) | async-done | bytes 524304 | tf_op jit(solution)/shard_map/psum | solution.py:28
  776.8 9.7 all-to-all-start.2
  786.5 48.8 %all-to-all-done.2 = f32[8,8,1,128,128]{3,1,4,2,0:T(8,128)} async-done(((f32[8,8,1,128,128]{3,1,4,2,0:T(8,128)}), f32[8,8,1,128,128]{3,1,4,2,0:T(8,128)}, u32[]{:S(2)}, u32[]{:S(2)}) %all-to-all-start.2) | async-done | bytes 4194336 | tf_op jit(solution)/shard_map/all_to_all | solution.py:13
  835.4 6.6 copy.187
  842.0 5.1 reshape_reshape.10
  848.9 11.7 %cholesky.252 = f32[128,128]{1,0:T(8,128)S(1)} custom-call(f32[128,128]{1,0:T(8,128)S(1)} %fusion.157), custom_call_target="Cholesky" | custom-call | tf_op jit(solution)/shard_map/jit(cholesky)/cholesky | solution.py:120
  861.9 9.8 custom-call.46
  871.7 5.4 convolution_select_fusion.1
  880.1 5.8 copy.214
  892.5 138.3 %all-reduce.6.cloned.1.call-done = f32[8,128,128]{2,1,0:T(8,128)} async-done(((f32[8,128,128]{2,1,0:T(8,128)}), f32[8,128,128]{2,1,0:T(8,128)}) %all-reduce.6.cloned.1.call-update) | async-done | bytes 524304 | tf_op jit(solution)/shard_map/psum | solution.py:28
  1036.1 10.1 all-to-all-start.3
  1046.3 5.1 fusion.57
  1051.3 43.7 %all-to-all-done.3 = f32[8,8,1,128,128]{3,1,4,2,0:T(8,128)} async-done(((f32[8,8,1,128,128]{3,1,4,2,0:T(8,128)}), f32[8,8,1,128,128]{3,1,4,2,0:T(8,128)}, u32[]{:S(2)}, u32[]{:S(2)}) %all-to-all-start.3) | async-done | bytes 4194336 | tf_op jit(solution)/shard_map/all_to_all | solution.py:13
  1095.1 6.6 copy.192
  1101.7 4.9 reshape_reshape.11
  1108.4 11.7 %cholesky.263 = f32[128,128]{1,0:T(8,128)S(1)} custom-call(f32[128,128]{1,0:T(8,128)S(1)} %fusion.155), custom_call_target="Cholesky" | custom-call | tf_op jit(solution)/shard_map/jit(cholesky)/cholesky | solution.py:120
  1121.5 9.8 custom-call.47
  1131.3 5.7 convolution_select_fusion
  1139.8 5.6 copy.215
  (202 shorter events, 156.8 us)
Async XLA Ops:
  7.2 211.0 %all-gather.2.cloned.1.call-start = ((), (), s32[]{:S(2)}) async-start(), calls=%async_computation.4 | async-start | bytes 17301504 | tf_op jit(solution)/shard_map/all_gather | solution.py:55
  68.9 177.4 %copy-start.15 = (pred[4096]{0:T(1024)(128)(4,1)}, pred[4096]{0:T(1024)(128)(4,1)S(1)}, u32[]{:S(2)}) copy-start(pred[4096]{0:T(1024)(128)(4,1)S(1)} %fusion.195) | copy-start | bytes 12292
  254.3 1.3 copy-start.5
  289.2 1.3 copy-start.6
  327.1 1.3 copy-start.12
  367.1 1.3 copy-start.13
  368.6 28.3 %copy-start.2 = (f32[3840,128]{0,1:T(8,128)S(1)}, f32[3840,128]{0,1:T(8,128)}, u32[]{:S(2)}) copy-start(f32[3840,128]{0,1:T(8,128)} %fusion.62) | copy-start | bytes 5898244
  396.9 4.4 copy-start.7
  401.3 4.3 copy-start.8
  405.6 4.2 copy-start.9
  547.8 19.0 %slice-start = ((s8[16777216]{0:T(1024)(128)(4,1)}), s8[4194304]{0:T(1024)(128)(4,1)S(1)}, s32[]{:S(2)}) async-start(s8[16777216]{0:T(1024)(128)(4,1)} %bitcast.210), calls=%async_computation.7 | async-start | bytes 8388608
  547.8 19.0 %slice-start.1 = ((s8[16777216]{0:T(1024)(128)(4,1)}), s8[4194304]{0:T(1024)(128)(4,1)S(1)}, s32[]{:S(2)}) async-start(s8[16777216]{0:T(1024)(128)(4,1)} %bitcast.210), calls=%async_computation.8 | async-start | bytes 8388608
  555.2 11.6 %slice-start.2 = ((s8[16777216]{0:T(1024)(128)(4,1)}), s8[4194304]{0:T(1024)(128)(4,1)S(1)}, s32[]{:S(2)}) async-start(s8[16777216]{0:T(1024)(128)(4,1)} %bitcast.210), calls=%async_computation.9 | async-start | bytes 8388608
  555.2 11.6 %slice-start.3 = ((s8[16777216]{0:T(1024)(128)(4,1)}), s8[4194304]{0:T(1024)(128)(4,1)S(1)}, s32[]{:S(2)}) async-start(s8[16777216]{0:T(1024)(128)(4,1)} %bitcast.210), calls=%async_computation.10 | async-start | bytes 8388608
  555.2 11.6 %copy-start.4 = (f32[1,4096,1,1,128]{4,3,2,1,0:T(1,128)S(1)}, f32[1,4096,1,1,128]{4,3,2,1,0:T(1,128)}, u32[]{:S(2)}) copy-start(f32[1,4096,1,1,128]{4,3,2,1,0:T(1,128)} %param.8) | copy-start | bytes 6291460
  591.4 1.4 copy-start.3
  591.4 1.4 slice-start.4
  595.6 8.0 copy-start.17
  595.6 28.4 %all-to-all-start.1 = ((f32[3,8,128,1,128]{4,2,0,3,1:T(8,128)}), f32[3,8,128,1,128]{4,2,0,3,1:T(8,128)}, u32[]{:S(2)}, u32[]{:S(2)}) async-start(f32[3,8,128,1,128]{4,2,0,3,1:T(8,128)} %copy.183), calls=%async_computation.1 | async-start | bytes 3145728 | tf_op jit(solution)/shard_map/all_to_all | solution.py:91
  603.2 170.1 %all-reduce.4.cloned.1.call-start = ((), (), s32[]{:S(2)}) async-start(), calls=%async_computation.5 | async-start | bytes 1048576 | tf_op jit(solution)/shard_map/psum | solution.py:28
  628.8 4.3 copy-start.14
  633.2 1.0 copy-start.10
  776.8 58.6 %all-to-all-start.2 = ((f32[8,8,1,128,128]{3,1,4,2,0:T(8,128)}), f32[8,8,1,128,128]{3,1,4,2,0:T(8,128)}, u32[]{:S(2)}, u32[]{:S(2)}) async-start(f32[8,8,1,128,128]{3,1,4,2,0:T(8,128)} %stack.6), calls=%async_computation.2 | async-start | bytes 8388608 | tf_op jit(solution)/shard_map/all_to_all | solution.py:13
  786.5 244.4 %all-reduce.6.cloned.1.call-start = ((), (), s32[]{:S(2)}) async-start(), calls=%async_computation.6 | async-start | bytes 1048576 | tf_op jit(solution)/shard_map/psum | solution.py:28
  877.2 1.9 copy-start.1
  880.0 8.6 copy-start.11
  1036.1 10.1 copy-start.16
  1036.1 58.9 %all-to-all-start.3 = ((f32[8,8,1,128,128]{3,1,4,2,0:T(8,128)}), f32[8,8,1,128,128]{3,1,4,2,0:T(8,128)}, u32[]{:S(2)}, u32[]{:S(2)}) async-start(f32[8,8,1,128,128]{3,1,4,2,0:T(8,128)} %stack.7), calls=%async_computation.3 | async-start | bytes 8388608 | tf_op jit(solution)/shard_map/all_to_all | solution.py:13
  1137.0 1.9 copy-start
Sparse Core Ops, SparseCore 0:
  68.9 149.1 all-gather.1
  635.2 138.0 all-reduce.3
  892.6 138.1 all-reduce.5
